TPU v7x, 32 devices: a whole 2x2x4 slice. The times are simulated.
32 devices in a mesh: prow: 8 (over z, y), pcol: 4 (over x, core).
Axes of the slice: x: 2, y: 2, z: 4, core: 2. Of those that a mesh axis runs over, the one named last changes fastest.
Arguments:
- inverse_tiles: bfloat16 [24576, 24576], P('prow', 'pcol'), may hold values from -6 to 6
- panel_blocks: bfloat16 [24576, 1536], P(('prow', 'pcol')), may hold values from -0.0546875 to 0.0546875
- pivot_inverse: bfloat16 [3, 512, 512], replicated, may hold values from -0.25 to 0.25
- diagonal_inverse: float32 [3, 512, 512], replicated, may hold values from -6 to 6
- ancestors: int32 [3, 24], replicated, may hold values from 0 to 47, all different within a row
Outputs:
- cross_blocks: float32 [24576, 1536], P(('prow', 'pcol'))
- diagonal_blocks: float32 [3, 512, 512], replicated
Inputs may be any that keep to these rules, and one draw needn't show every extreme that they name: `ancestors`: each row names 24 different blocks, and every block is named by some row.
All inputs are finite; a program needn't handle non-finite values.
Results may differ from a plain program's by a relative error of at most 0.003.
Values may be sent and summed in bfloat16 or wider, within the bound.
A program may use at most 128 MiB of HBM per device.

v0:
```python
import jax
import jax.numpy as jnp
from jax import lax
from jax.sharding import PartitionSpec as P


def spread(value, axis, source):
    kept = jnp.where(lax.axis_index(axis) == source, value, 0).astype(value.dtype)
    return lax.psum(kept, axis)


def row_terms(inverse_tiles, columns):
    return jnp.dot(inverse_tiles, columns, preferred_element_type=jnp.float32)


def on_device(inverse_tiles, panel_blocks, pivot_inverse, diagonal_inverse, ancestors):
    seg_rows = panel_blocks.shape[0]
    n_super = pivot_inverse.shape[0]
    width = pivot_inverse.shape[1]
    row_devices = lax.axis_size("prow")
    col_devices = lax.axis_size("pcol")
    segment = lax.axis_index("prow") * col_devices + lax.axis_index("pcol")
    row_ids = segment * seg_rows + lax.iota(jnp.int32, seg_rows)
    block_ids = row_ids // width
    listed = jnp.any(block_ids[:, None, None] == ancestors[None, :, :], axis=2).astype(jnp.float32)
    raw_three = panel_blocks.reshape(seg_rows, n_super, width)
    normed = jnp.einsum(
        "rsw,swv->rsv", raw_three, pivot_inverse, preferred_element_type=jnp.float32
    )
    scaled = (normed * listed[:, :, None]).astype(jnp.bfloat16)
    own_panel = scaled.reshape(seg_rows, n_super * width)
    row_panel = lax.all_gather(own_panel, "pcol", axis=0, tiled=True)
    ratio = row_devices // col_devices
    pieces = []
    for offset in range(ratio):
        pieces.append(spread(row_panel, "prow", lax.axis_index("pcol") * ratio + offset))
    column_panel = jnp.concatenate(pieces, axis=0)
    summed = lax.psum_scatter(
        row_terms(inverse_tiles, column_panel), "pcol", scatter_dimension=0, tiled=True
    )
    cross = -(summed.reshape(seg_rows, n_super, width) * listed[:, :, None])
    local_terms = jnp.einsum(
        "rsw,rsv->swv", scaled.astype(jnp.float32), cross, precision=lax.Precision.HIGHEST
    )
    total = lax.psum(local_terms, ("prow", "pcol"))
    diagonal = diagonal_inverse - total
    return (cross.reshape(seg_rows, n_super * width), diagonal)


def solution(mesh):
    in_specs = (P("prow", "pcol"), P(("prow", "pcol"), None), P(), P(), P())
    out_specs = (P(("prow", "pcol"), None), P())
    return jax.shard_map(
        on_device, mesh=mesh, in_specs=in_specs, out_specs=out_specs, check_vma=False
    )
```

profile of v0, /device:TPU:0, one launch (start us, length us, event | category | flops | bytes accessed | tf_op | source)
XLA Modules:
  0.0 1028.7 jit_solution(8723417123079161685)
XLA Ops:
  7.2 0.0 copy-start
  7.2 0.0 all-gather.2.cloned.1.call-start
  7.3 0.9 compare_reduce_fusion
  8.2 0.0 copy-start.2
  8.2 4.3 copy.16
  12.4 0.0 copy-done
  12.4 4.5 fusion.8
  17.0 0.0 copy-done.2
  17.0 0.0 all-gather.2.cloned.1.call-update
  17.0 0.0 all-reduce.6.cloned.1.call-start
  17.0 67.0 %all-gather.2.cloned.1.call-done = bf16[3072,1536]{0,1:T(8,128)(2,1)} async-done(((bf16[768,1536]{0,1:T(8,128)(2,1)}), bf16[3072,1536]{0,1:T(8,128)(2,1)}) %all-gather.2.cloned.1.call-update) | async-done | bytes 9437200 | tf_op jit(solution)/shard_map/all_gather | solution.py:32
  84.1 10.7 %broadcast_select_fusion.1 = (bf16[3072,1536]{0,1:T(8,128)(2,1)}, bf16[3072,1536]{0,1:T(8,128)(2,1)}) fusion(bf16[3072,1536]{0,1:T(8,128)(2,1)} %all-gather.2.cloned.1.call-done, pred[]{:T(512)S(6)} %eq.19, pred[]{:T(512)S(6)} %eq.23), kind=kLoop, calls=%fused_computation.6 | loop fusion | flops 9437184 | bytes 28311554 | tf_op jit(solution)/shard_map/jit(_where)/select_n | solution.py:8
  94.8 0.0 all-reduce.6.cloned.1.call-update
  94.8 0.0 reduce-scatter.2.cloned.1.call-start
  94.9 567.5 %all-reduce.6.cloned.1.call-done = (bf16[3072,1536]{0,1:T(8,128)(2,1)}, bf16[3072,1536]{0,1:T(8,128)(2,1)}) async-done(((bf16[3072,1536]{0,1:T(8,128)(2,1)}, bf16[3072,1536]{0,1:T(8,128)(2,1)}), (bf16[3072,1536]{0,1:T(8,128)(2,1)}, bf16[3072,1536]{0,1:T(8,128)(2,1)})) %all-reduce.6.cloned.1.call-update) | async-done | bytes 18874384 | tf_op jit(solution)/shard_map/psum | solution.py:9
  662.4 70.5 %fusion.4 = f32[3072,1536]{0,1:T(8,128)} fusion(bf16[3072,6144]{1,0:T(8,128)(2,1)} %param.5, bf16[3072,1536]{0,1:T(8,128)(2,1)} %get-tuple-element.8, bf16[3072,1536]{0,1:T(8,128)(2,1)} %get-tuple-element.9), kind=kOutput, calls=%fused_computation.4 | convolution fusion | flops 58019807232 | bytes 75497472 | tf_op jit(solution)/shard_map/dot_general | solution.py:13
  732.9 0.0 copy-start.3
  732.9 0.0 reduce-scatter.2.cloned.1.call-update
  732.9 0.2 all-reduce.4.cloned.1.call-start
  733.2 136.7 %reduce-scatter.2.cloned.1.call-done = f32[768,1536]{0,1:T(8,128)} async-done(((f32[3072,1536]{0,1:T(8,128)}), f32[768,1536]{0,1:T(8,128)}) %reduce-scatter.2.cloned.1.call-update) | async-done | bytes 4718608 | tf_op jit(solution)/shard_map/reduce_scatter | solution.py:38
  869.8 0.0 copy-done.3
  869.8 8.8 fusion.9
  878.6 0.0 all-reduce.4.cloned.1.call-update
  878.6 4.8 fusion.7
  883.4 0.0 copy-start.1
  883.4 6.4 copy.20
  889.9 127.0 %all-reduce.4.cloned.1.call-done = f32[3,512,512]{2,1,0:T(8,128)} async-done(((f32[3,512,512]{2,1,0:T(8,128)}), f32[3,512,512]{2,1,0:T(8,128)}) %all-reduce.4.cloned.1.call-update) | async-done | bytes 3145744 | tf_op jit(solution)/shard_map/psum | solution.py:45
  1016.9 5.3 sub.10
  1022.2 0.0 copy-done.1
  (2 shorter events, 0.0 us)
Async XLA Ops:
  7.2 5.3 copy-start
  7.2 76.9 %all-gather.2.cloned.1.call-start = ((), (), s32[]{:S(2)}) async-start(), calls=%async_computation.1 | async-start | bytes 11796480 | tf_op jit(solution)/shard_map/all_gather | solution.py:32
  8.2 8.8 copy-start.2
  17.0 645.4 %all-reduce.6.cloned.1.call-start = ((), (), s32[]{:S(2)}) async-start(), calls=%async_computation.4 | async-start | bytes 37748736 | tf_op jit(solution)/shard_map/psum | solution.py:9
  94.8 775.0 %reduce-scatter.2.cloned.1.call-start = ((), (), s32[]{:S(2)}) async-start(), calls=%async_computation.2 | async-start | bytes 23592960 | tf_op jit(solution)/shard_map/reduce_scatter | solution.py:38
  732.9 136.9 %copy-start.3 = (f32[768,3]{0,1:T(4,128)S(1)}, f32[768,3]{0,1:T(4,128)}, u32[]{:S(2)}) copy-start(f32[768,3]{0,1:T(4,128)} %copy-done.2) | copy-start | bytes 27652
  732.9 284.0 %all-reduce.4.cloned.1.call-start = ((), (), s32[]{:S(2)}) async-start(), calls=%async_computation.3 | async-start | bytes 6291456 | tf_op jit(solution)/shard_map/psum | solution.py:45
  883.4 138.7 %copy-start.1 = (bf16[3,512,512]{2,1,0:T(8,128)(2,1)S(1)}, bf16[3,512,512]{2,1,0:T(8,128)(2,1)}, u32[]{:S(2)}) copy-start(bf16[3,512,512]{2,1,0:T(8,128)(2,1)} %param.7) | copy-start | bytes 4718596
Sparse Core Ops, SparseCore 0:
  17.1 66.9 all-gather.1
  94.9 567.4 all-reduce.5
  733.0 136.7 reduce-scatter.1
  878.8 138.0 all-reduce.3
where the time goes:
time: 1030 us
  waiting for transfers between devices  898 us (87%)
  matrix products  83.8 us (8%)
  other arithmetic  21.7 us (2%)
  between operations  13.8 us (1%)
  local copies, waits for them, and re-layouts  10.7 us (1%)
    psum x1, waiting for transfers between devices, spread(): return lax.psum(kept, axis)  568 us
    reduce_scatter x1, waiting for transfers between devices, on_device(): lax.psum_scatter(row_terms(inverse_tiles, column_panel), 'pcol', scatter_...  137 us
    psum x1, waiting for transfers between devices, on_device(): total = lax.psum(local_terms, ('prow', 'pcol'))  127 us
    dot_general x1, matrix products, row_terms(): return jnp.dot(inverse_tiles, columns, preferred_element_type=jnp.float32)  70.5 us
    all_gather x1, waiting for transfers between devices, on_device(): row_panel = lax.all_gather(own_panel, 'pcol', axis=0, tiled=True)  67 us
  transfers between devices with their start and end apart: 4, of which 4 were waited for; matrix products, arithmetic and copies ran while one was open for 1% of the time, Pallas kernels for 0%

commit v1 on v0

--- a/solution.py
+++ b/solution.py
@@ -29,7 +29,16 @@
     )
     scaled = (normed * listed[:, :, None]).astype(jnp.bfloat16)
     own_panel = scaled.reshape(seg_rows, n_super * width)
-    row_panel = lax.all_gather(own_panel, "pcol", axis=0, tiled=True)
+    ways = lax.axis_size("pcol")
+    up = [(d, (d + 1) % ways) for d in range(ways)]
+    down = [(d, (d - 1) % ways) for d in range(ways)]
+    earlier, later = ([own_panel], [own_panel])
+    for _ in range(ways // 2):
+        earlier.append(lax.ppermute(earlier[-1], "pcol", up))
+    for _ in range((ways - 1) // 2):
+        later.append(lax.ppermute(later[-1], "pcol", down))
+    line = jnp.concatenate([*earlier[::-1], *later[1:]], axis=0)
+    row_panel = jnp.roll(line, (lax.axis_index("pcol") - ways // 2) * own_panel.shape[0], axis=0)
     ratio = row_devices // col_devices
     pieces = []
     for offset in range(ratio):

time: 1030 us -> 1060 us (1.029)
  local copies, waits for them, and re-layouts: 10.7 us -> 26.5 us
  waiting for transfers between devices: 898 us -> 913 us
    ppermute x0 -> x3, waiting for transfers between devices: none -> 78.3 us  [the longest x2 78.3 us: on_device(): earlier.append(lax.ppermute(earlier[-1], 'pcol', up))]
    all_gather x1 -> x0, waiting for transfers between devices: 67 us -> none  [on_device(): row_panel = lax.all_gather(own_panel, 'pcol', axis=0, tiled=True)]
    unnamed x10 -> x17, local copies, waits for them, and re-layouts: 10.7 us -> 24.5 us
  transfers between devices with their start and end apart: 4 -> 6, of which waited for: 4 -> 5; matrix products, arithmetic and copies ran while one was open for 1% -> 2% of each run, Pallas kernels for 0% -> 0%
where the time goes in v1:
time: 1060 us
  waiting for transfers between devices  913 us (86%)
  matrix products  83.8 us (8%)
  local copies, waits for them, and re-layouts  26.5 us (2%)
  other arithmetic  20.8 us (2%)
  between operations  13.9 us (1%)
    psum x1, waiting for transfers between devices, spread(): return lax.psum(kept, axis)  571 us
    reduce_scatter x1, waiting for transfers between devices, on_device(): lax.psum_scatter(row_terms(inverse_tiles, column_panel), 'pcol', scatter_...  137 us
    psum x1, waiting for transfers between devices, on_device(): total = lax.psum(local_terms, ('prow', 'pcol'))  127 us
    ppermute x2, waiting for transfers between devices, on_device(): earlier.append(lax.ppermute(earlier[-1], 'pcol', up))  78.3 us
    dot_general x1, matrix products, row_terms(): return jnp.dot(inverse_tiles, columns, preferred_element_type=jnp.float32)  70.5 us
    unnamed x17, local copies, waits for them, and re-layouts  24.5 us
  transfers between devices with their start and end apart: 6, of which 5 were waited for; matrix products, arithmetic and copies ran while one was open for 2% of the time, Pallas kernels for 0%

profile of v1, /device:TPU:0, one launch (start us, length us, event | category | flops | bytes accessed | tf_op | source)
XLA Modules:
  0.0 1060.8 jit_solution(7966347351701540537)
XLA Ops:
  7.2 0.0 copy-start
  7.2 0.0 all-reduce.6.cloned.1.call-start
  7.2 0.9 compare_reduce_fusion
  8.2 4.3 copy.16
  12.4 4.5 fusion.8
  17.0 0.5 collective-permute-start
  17.4 28.8 %collective-permute-done = bf16[768,1536]{0,1:T(8,128)(2,1)} collective-permute-done((bf16[768,1536]{0,1:T(8,128)(2,1)}, bf16[768,1536]{0,1:T(8,128)(2,1)}, u32[]{:S(2)}, u32[]{:S(2)}) %collective-permute-start) | collective-permute-done | bytes 2359328 | tf_op jit(solution)/shard_map/ppermute | solution.py:37
  46.2 1.7 collective-permute-start.2
  48.0 49.5 %collective-permute-done.1 = bf16[768,1536]{0,1:T(8,128)(2,1)} collective-permute-done((bf16[768,1536]{0,1:T(8,128)(2,1)}, bf16[768,1536]{0,1:T(8,128)(2,1)}, u32[]{:S(2)}, u32[]{:S(2)}) %collective-permute-start.1) | collective-permute-done | bytes 2359328 | tf_op jit(solution)/shard_map/ppermute | solution.py:37
  97.5 2.0 constant_dynamic-update-slice_fusion.7
  99.5 2.0 constant_dynamic-update-slice_fusion.6
  101.5 2.0 constant_dynamic-update-slice_fusion.5
  103.5 2.0 constant_dynamic-update-slice_fusion.4
  105.5 2.0 constant_dynamic-update-slice_fusion.3
  107.5 2.0 constant_dynamic-update-slice_fusion.2
  109.5 2.0 constant_dynamic-update-slice_fusion.1
  111.5 2.0 constant_dynamic-update-slice_fusion
  113.5 9.7 broadcast_select_fusion.1
  123.2 0.0 all-reduce.6.cloned.1.call-update
  123.2 0.2 reduce-scatter.2.cloned.1.call-start
  123.4 571.1 %all-reduce.6.cloned.1.call-done = (bf16[3072,1536]{0,1:T(8,128)(2,1)}, bf16[3072,1536]{0,1:T(8,128)(2,1)}) async-done(((bf16[3072,1536]{0,1:T(8,128)(2,1)}, bf16[3072,1536]{0,1:T(8,128)(2,1)}), (bf16[3072,1536]{0,1:T(8,128)(2,1)}, bf16[3072,1536]{0,1:T(8,128)(2,1)})) %all-reduce.6.cloned.1.call-update) | async-done | bytes 18874384 | tf_op jit(solution)/shard_map/psum | solution.py:9
  694.5 70.5 %fusion.4 = f32[3072,1536]{0,1:T(8,128)} fusion(bf16[3072,6144]{1,0:T(8,128)(2,1)} %param.5, bf16[3072,1536]{0,1:T(8,128)(2,1)} %get-tuple-element.8, bf16[3072,1536]{0,1:T(8,128)(2,1)} %get-tuple-element.9), kind=kOutput, calls=%fused_computation.4 | convolution fusion | flops 58019807232 | bytes 75497472 | tf_op jit(solution)/shard_map/dot_general | solution.py:13
  765.0 0.0 reduce-scatter.2.cloned.1.call-update
  765.1 0.3 all-reduce.4.cloned.1.call-start
  765.3 136.6 %reduce-scatter.2.cloned.1.call-done = f32[768,1536]{0,1:T(8,128)} async-done(((f32[3072,1536]{0,1:T(8,128)}), f32[768,1536]{0,1:T(8,128)}) %reduce-scatter.2.cloned.1.call-update) | async-done | bytes 4718608 | tf_op jit(solution)/shard_map/reduce_scatter | solution.py:47
  902.0 8.8 fusion.9
  910.7 0.0 all-reduce.4.cloned.1.call-update
  910.8 0.0 copy-start.1
  910.8 4.9 fusion.7
  915.7 6.3 copy.20
  922.0 127.1 %all-reduce.4.cloned.1.call-done = f32[3,512,512]{2,1,0:T(8,128)} async-done(((f32[3,512,512]{2,1,0:T(8,128)}), f32[3,512,512]{2,1,0:T(8,128)}) %all-reduce.4.cloned.1.call-update) | async-done | bytes 3145744 | tf_op jit(solution)/shard_map/psum | solution.py:54
  1049.0 5.3 sub.19
  (10 shorter events, 0.0 us)
Async XLA Ops:
  7.2 5.3 copy-start
  7.2 687.4 %all-reduce.6.cloned.1.call-start = ((), (), s32[]{:S(2)}) async-start(), calls=%async_computation.3 | async-start | bytes 37748736 | tf_op jit(solution)/shard_map/psum | solution.py:9
  8.2 93.3 %copy-start.2 = (f32[768,3]{0,1:T(4,128)}, f32[768,3]{0,1:T(4,128)S(1)}, u32[]{:S(2)}) copy-start(f32[768,3]{0,1:T(4,128)S(1)} %convert_element_type.14) | copy-start | bytes 27652
  17.0 29.2 %collective-permute-start = (bf16[768,1536]{0,1:T(8,128)(2,1)}, bf16[768,1536]{0,1:T(8,128)(2,1)}, u32[]{:S(2)}, u32[]{:S(2)}) collective-permute-start(bf16[768,1536]{0,1:T(8,128)(2,1)} %bitcast.2), channel_id=1, source_target_pairs={{0,1},{1,2},{2,3},{3,0},{4,5},{5,6},{6,7},{7,4},{8,9},{9,10},{10,1... | collective-permute-start | bytes 7077896 | tf_op jit(solution)/shard_map/ppermute | solution.py:37
  46.2 51.3 %collective-permute-start.1 = (bf16[768,1536]{0,1:T(8,128)(2,1)}, bf16[768,1536]{0,1:T(8,128)(2,1)}, u32[]{:S(2)}, u32[]{:S(2)}) collective-permute-start(bf16[768,1536]{0,1:T(8,128)(2,1)} %collective-permute-done), channel_id=1, source_target_pairs={{0,1},{1,2},{2,3},{3,0},{4,5},{5,6},{6,7},{7,4},{8,9},{9,10},{10,1... | collective-permute-start | bytes 7077896 | tf_op jit(solution)/shard_map/ppermute | solution.py:37
  46.2 57.3 %collective-permute-start.2 = (bf16[768,1536]{0,1:T(8,128)(2,1)}, bf16[768,1536]{0,1:T(8,128)(2,1)}, u32[]{:S(2)}, u32[]{:S(2)}) collective-permute-start(bf16[768,1536]{0,1:T(8,128)(2,1)} %bitcast.2), channel_id=1, source_target_pairs={{0,3},{1,0},{2,1},{3,2},{4,7},{5,4},{6,5},{7,6},{8,11},{9,8},{10,9... | collective-permute-start | bytes 7077896 | tf_op jit(solution)/shard_map/ppermute | solution.py:39
  123.2 778.8 %reduce-scatter.2.cloned.1.call-start = ((), (), s32[]{:S(2)}) async-start(), calls=%async_computation.1 | async-start | bytes 23592960 | tf_op jit(solution)/shard_map/reduce_scatter | solution.py:47
  765.0 136.9 %copy-start.3 = (f32[768,3]{0,1:T(4,128)S(1)}, f32[768,3]{0,1:T(4,128)}, u32[]{:S(2)}) copy-start(f32[768,3]{0,1:T(4,128)} %copy-done.2) | copy-start | bytes 27652
  765.1 284.0 %all-reduce.4.cloned.1.call-start = ((), (), s32[]{:S(2)}) async-start(), calls=%async_computation.2 | async-start | bytes 6291456 | tf_op jit(solution)/shard_map/psum | solution.py:54
  910.8 143.5 %copy-start.1 = (bf16[3,512,512]{2,1,0:T(8,128)(2,1)S(1)}, bf16[3,512,512]{2,1,0:T(8,128)(2,1)}, u32[]{:S(2)}) copy-start(bf16[3,512,512]{2,1,0:T(8,128)(2,1)} %param.7) | copy-start | bytes 4718596
Sparse Core Ops, SparseCore 0:
  123.3 571.2 all-reduce.5
  765.2 136.7 reduce-scatter.1
  910.9 138.1 all-reduce.3
